TPU v7x, 32 devices: a whole 2x2x4 slice. The times are simulated.
32 devices in a mesh: dp: 4 (over z), section: 2 (over core), tensor: 4 (over y, x).
Axes of the slice: x: 2, y: 2, z: 4, core: 2. Of those that a mesh axis runs over, the one named last changes fastest.
Arguments:
- tokens: bfloat16 [1024, 8192], P('dp', 'tensor'), may hold values from -6 to 6
- dest_slot: int32 [1024], P('dp'), may hold values from 0 to 1023, as said below
- doc_reset: int32 [1024], P('dp'), may hold values 0 or 1
- norm_gain: float32 [2, 8192], P('section'), may hold values from 0.25 to 1.75
- w_in: bfloat16 [2, 8192, 5120], P('section', 'dp', 'tensor'), may hold values from -0.0625 to 0.0625
- w_step: bfloat16 [2, 8192, 32], P('section', None, 'tensor'), may hold values from -0.0625 to 0.0625
- step_bias: float32 [2, 32], P('section', 'tensor'), may hold values from -4 to -1.5
- a_log: float32 [2, 32], P('section', 'tensor'), may hold values from -2.5 to 1.5
- d_skip: float32 [2, 32], P('section', 'tensor'), may hold values from 0.3 to 2
- out_gain: float32 [2, 2048], P('section', 'tensor'), may hold values from 0.25 to 1.75
- w_out: bfloat16 [2, 2048, 8192], P('section', 'tensor'), may hold values from -0.125 to 0.125
Outputs:
- phase_out: bfloat16 [2, 1024, 8192], P('section', 'dp', 'tensor')
Inputs may be any that keep to these rules, and one draw needn't show every extreme that they name: dest_slot is a permutation; the tokens of one group go in order to increasing groups, and each group receives rows in order of source group. One group sends at most 128 tokens to one group, and every group sends exactly 128 to some group.
All inputs are finite; a program needn't handle non-finite values. No bound on the sum of `doc_reset` on one device may be relied on, other than what follows from the above.
Results may differ from a plain program's by a relative error of at most 0.018.
Values may be sent and summed in bfloat16 or wider, within the bound.
A program may use at most 128 MiB of HBM per device.

v0:
```python
import jax
import jax.numpy as jnp
from jax import lax
from jax.sharding import PartitionSpec as P

HEAD_DIM = 64
STATE = 128
HEADS_DEV = 8
SPAN = 64
epsilon = 1e-05


def scan_block(inputs, writes, readout, step_size, log_decay, resets, state, skips):
    segment = jnp.cumsum(resets)
    cumulative = jnp.cumsum(log_decay, axis=0)
    positions = jnp.arange(resets.shape[0])
    in_segment = (segment[:, None] == segment[None, :]) & (positions[:, None] >= positions[None, :])
    by_head = cumulative.T
    gap = by_head[:, :, None] - by_head[:, None, :]
    decayed = jnp.where(in_segment[None], jnp.exp(jnp.where(in_segment[None], gap, 0.0)), 0.0)
    f32 = jnp.float32
    scores = jnp.einsum("tn,sn->ts", readout, writes, preferred_element_type=f32)
    weights = scores[None] * decayed * step_size.T[:, None, :]
    output = jnp.einsum("hts,shp->thp", weights, inputs.astype(f32))
    carry_ok = (segment == 0).astype(f32)
    carried = jnp.einsum("tn,hpn->thp", readout.astype(f32), state)
    output = output + carry_ok[:, None, None] * jnp.exp(cumulative)[:, :, None] * carried
    last_seg = segment[-1]
    tail = (
        (segment == last_seg).astype(f32)[:, None]
        * jnp.exp(cumulative[-1][None, :] - cumulative)
        * step_size
    )
    fresh = jnp.einsum("shp,sn->hpn", tail[:, :, None] * inputs.astype(f32), writes.astype(f32))
    kept = (last_seg == 0).astype(f32) * jnp.exp(cumulative[-1])[:, None, None] * state
    output = output + skips[None, :, None] * inputs.astype(f32)
    return (output, fresh + kept)


def per_device(
    tokens, dest_slot, doc_reset, norm_gain, w_in, w_step, step_bias, a_log, d_skip, out_gain, w_out
):
    f32, bf16 = (jnp.float32, jnp.bfloat16)
    groups = lax.axis_size("dp")
    width = lax.axis_size("tensor")
    cores = lax.axis_size("section")
    layers = cores
    dp_idx = lax.axis_index("dp")
    core = lax.axis_index("section")
    row_count = tokens.shape[0]
    feat_local = tokens.shape[1]
    feats = feat_local * width
    capacity = 2 * row_count // groups
    head_cols = HEADS_DEV * HEAD_DIM

    def whole(param):
        return lax.all_gather(param, "section", axis=0, tiled=True)

    w_in, w_out, w_step = (whole(w_in), whole(w_out), whole(w_step))
    norm_gain, step_bias, a_log, d_skip, out_gain = (
        whole(norm_gain),
        whole(step_bias),
        whole(a_log),
        whole(d_skip),
        whole(out_gain),
    )
    part = feat_local // cores
    mine = lax.dynamic_slice_in_dim(tokens, core * part, part, axis=1)
    target = dest_slot // row_count
    onehot = (target[:, None] == jnp.arange(groups)[None, :]).astype(jnp.int32)
    before = jnp.cumsum(onehot, axis=0) - onehot
    placed = jnp.sum(onehot * before, axis=1)
    slots = target * capacity + placed
    outbox = jnp.zeros((groups * capacity, part), bf16).at[slots].set(mine)
    marks = (
        jnp.full((groups * capacity,), row_count, jnp.int32).at[slots].set(dest_slot % row_count)
    )
    inbox = lax.all_to_all(
        outbox.reshape(groups, capacity, part), "dp", split_axis=0, concat_axis=0, tiled=True
    )
    where_to = lax.all_to_all(
        marks.reshape(groups, capacity), "dp", split_axis=0, concat_axis=0, tiled=True
    )
    balanced = (
        jnp.zeros((row_count, part), bf16)
        .at[where_to.reshape(-1)]
        .set(inbox.reshape(-1, part), mode="drop")
    )
    few = row_count // (cores * width)
    half = row_count // cores
    rows = lax.all_to_all(
        balanced.reshape(cores * width, few, part), ("section", "tensor"), 0, 0, tiled=True
    )
    rows = rows.reshape(cores, width, few, part).transpose(2, 1, 0, 3).reshape(few, feats)
    depth = w_in.shape[1]
    outs = []
    for layer in range(layers):
        widened = rows.astype(f32)
        meansq = jnp.mean(widened * widened, axis=-1, keepdims=True)
        u = (widened * lax.rsqrt(meansq + epsilon) * norm_gain[layer]).astype(bf16)
        u = u.reshape(few, groups, depth).transpose(1, 0, 2)
        u = lax.all_to_all(u, "dp", 0, 0, tiled=True)
        step_w = lax.dynamic_slice_in_dim(w_step[layer], dp_idx * depth, depth, axis=0)
        full_u = lax.all_gather(u, "tensor", axis=1, tiled=True)
        full_u = full_u.reshape(groups * half, depth)
        proj = jnp.dot(full_u, w_in[layer], preferred_element_type=f32).astype(bf16)
        pre = jnp.dot(full_u, step_w, preferred_element_type=f32)
        proj = lax.all_to_all(proj.reshape(groups, half, -1), "dp", 0, 0, tiled=True)
        pre = lax.all_to_all(pre.reshape(groups, half, HEADS_DEV), "dp", 0, 0, tiled=True)
        proj = jnp.sum(proj.astype(f32), axis=0).astype(bf16)
        pre = jnp.sum(pre, axis=0)
        proj = lax.all_gather(proj, "section", axis=0, tiled=True)
        pre = lax.all_gather(pre, "section", axis=0, tiled=True)
        step_size = jax.nn.softplus(pre + step_bias[layer])
        log_decay = -jnp.exp(a_log[layer]) * step_size
        state = jnp.zeros((HEADS_DEV, HEAD_DIM, STATE), f32)
        mixed = []
        for at in range(0, row_count, SPAN):
            span = slice(at, at + SPAN)
            output, state = scan_block(
                proj[span, head_cols : 2 * head_cols].reshape(SPAN, HEADS_DEV, HEAD_DIM),
                proj[span, 2 * head_cols : 2 * head_cols + STATE],
                proj[span, 2 * head_cols + STATE :],
                step_size[span],
                log_decay[span],
                doc_reset[span],
                state,
                d_skip[layer],
            )
            mixed.append(output.reshape(SPAN, head_cols))
        mixed = jnp.concatenate(mixed, axis=0)
        mixed = lax.dynamic_slice_in_dim(mixed, core * half, half, axis=0)
        gate = lax.dynamic_slice_in_dim(proj[:, :head_cols], core * half, half, axis=0).astype(f32)
        gated = mixed * jax.nn.silu(gate)
        meansq_out = jnp.mean(gated * gated, axis=-1, keepdims=True)
        normed = (gated * lax.rsqrt(meansq_out + epsilon) * out_gain[layer]).astype(bf16)
        partial_value = jnp.dot(normed, w_out[layer], preferred_element_type=f32).astype(bf16)
        partial_value = lax.all_to_all(
            partial_value.reshape(width, few, feats), "tensor", 0, 0, tiled=True
        )
        summed = jnp.sum(partial_value.astype(f32), axis=0)
        rows = (widened + summed).astype(bf16)
        outs.append(rows.reshape(few, width, feat_local).transpose(1, 0, 2))
    outs = jnp.concatenate(outs, axis=0)
    outs = lax.all_to_all(outs, ("section", "tensor"), 0, 0, tiled=True)
    return outs.reshape(1, row_count, feat_local)


def solution(mesh):
    placed = (
        P("dp", "tensor"),
        P("dp"),
        P("dp"),
        P("section", None),
        P("section", "dp", "tensor"),
        P("section", None, "tensor"),
        P("section", "tensor"),
        P("section", "tensor"),
        P("section", "tensor"),
        P("section", "tensor"),
        P("section", "tensor", None),
    )
    return jax.shard_map(
        per_device,
        mesh=mesh,
        in_specs=placed,
        out_specs=P("section", "dp", "tensor"),
        check_vma=False,
    )
```

profile of v0, /device:TPU:0, one launch (start us, length us, event | category | flops | bytes accessed | tf_op | source)
XLA Modules:
  0.0 413.6 jit_solution(3138068230953162979)
XLA Ops:
  10.9 6.3 %all-to-all-start = ((s32[4,1,128]{2,1,0:T(1,128)}), s32[4,1,128]{2,1,0:T(1,128)S(1)}, u32[]{:S(2)}, u32[]{:S(2)}) async-start(s32[4,1,128]{2,1,0:T(1,128)} %bitcast.3), calls=%async_computation | async-start | bytes 4096 | tf_op jit(solution)/shard_map/all_to_all | solution.py:81
  17.3 2.6 scatter_custom_fusion.1
  19.9 2.8 all-to-all-done
  22.7 3.5 all-to-all-start.1
  26.3 24.7 %all-to-all-done.1 = bf16[4,128,1024]{2,1,0:T(8,128)(2,1)S(1)} async-done(((bf16[4,128,1024]{2,1,0:T(8,128)(2,1)}), bf16[4,128,1024]{2,1,0:T(8,128)(2,1)S(1)}, u32[]{:S(2)}, u32[]{:S(2)}) %all-to-all-start.1) | async-done | bytes 1048608 | tf_op jit(solution)/shard_map/all_to_all | solution.py:78
  50.9 3.4 scatter_custom_fusion.2
  54.4 3.7 all-to-all-start.2
  60.8 6.4 %all-to-all-done.2 = bf16[8,32,1024]{2,1,0:T(8,128)(2,1)S(1)} async-done(((bf16[8,32,1024]{2,1,0:T(8,128)(2,1)}), bf16[8,32,1024]{2,1,0:T(8,128)(2,1)S(1)}, u32[]{:S(2)}, u32[]{:S(2)}) %all-to-all-start.2) | async-done | bytes 524320 | tf_op jit(solution)/shard_map/all_to_all | solution.py:91
  67.9 18.4 %all_to_all.64 = bf16[4,32,2048]{2,1,0:T(8,128)(2,1)} all-to-all(bf16[4,32,2048]{2,1,0:T(8,128)(2,1)S(1)} %fusion.28), channel_id=1, replica_groups=mesh['dp'=4,'section'=2,'tensor'=4] {'dp'}, dimensions={0} | all-to-all | bytes 1048576 | tf_op jit(solution)/shard_map/all_to_all | solution.py:102
  107.1 12.1 %all-gather.10.cloned.1.call-done = bf16[4,128,2048]{2,1,0:T(8,128)(2,1)} async-done(((bf16[4,32,2048]{2,1,0:T(8,128)(2,1)}), bf16[4,128,2048]{2,1,0:T(8,128)(2,1)}) %all-gather.10.cloned.1.call-update) | async-done | bytes 2097168 | tf_op jit(solution)/shard_map/all_gather | solution.py:104
  119.2 2.9 fusion.166
  122.0 4.6 %all-to-all-start.5 = ((f32[4,128,8]{1,2,0:T(8,128)}), f32[4,128,8]{1,2,0:T(8,128)S(1)}, u32[]{:S(2)}, u32[]{:S(2)}) async-start(f32[4,128,8]{1,2,0:T(8,128)} %fusion.166), calls=%async_computation.5 | async-start | bytes 32768 | tf_op jit(solution)/shard_map/all_to_all | solution.py:109
  128.5 3.8 all-to-all-done.5
  136.1 7.3 %all-gather.12.cloned.1.call-done = bf16[2,2048,1280]{2,1,0:T(8,128)(2,1)} async-done(((bf16[1,2048,1280]{2,1,0:T(8,128)(2,1)}), bf16[2,2048,1280]{2,1,0:T(8,128)(2,1)}) %all-gather.12.cloned.1.call-update) | async-done | bytes 10485776 | tf_op jit(solution)/shard_map/all_gather | solution.py:57
  143.4 7.1 %fusion.2 = bf16[512,1280]{1,0:T(8,128)(2,1)} fusion(bf16[512,2048]{1,0:T(8,128)(2,1)} %bitcast.275, bf16[2,2048,1280]{2,1,0:T(8,128)(2,1)} %all-gather.12.cloned.1.call-done), kind=kOutput, calls=%fused_computation.13 | convolution fusion | flops 2685009920 | bytes 8650752 | tf_op jit(solution)/shard_map/dot_general | solution.py:106
  150.5 4.9 %all-to-all-start.4 = ((bf16[4,128,1280]{2,1,0:T(8,128)(2,1)}), bf16[4,128,1280]{2,1,0:T(8,128)(2,1)}, u32[]{:S(2)}, u32[]{:S(2)}) async-start(bf16[4,128,1280]{2,1,0:T(8,128)(2,1)} %bitcast.280), calls=%async_computation.4 | async-start | bytes 2621440 | tf_op jit(solution)/shard_map/all_to_all | solution.py:108
  159.4 27.9 %all-to-all-done.4 = bf16[4,128,1280]{2,1,0:T(8,128)(2,1)} async-done(((bf16[4,128,1280]{2,1,0:T(8,128)(2,1)}), bf16[4,128,1280]{2,1,0:T(8,128)(2,1)}, u32[]{:S(2)}, u32[]{:S(2)}) %all-to-all-start.4) | async-done | bytes 1310752 | tf_op jit(solution)/shard_map/all_to_all | solution.py:108
  188.8 2.5 all_gather.45
  205.0 6.0 %convolution_convert_fusion.1 = bf16[128,8192]{1,0:T(8,128)(2,1)} fusion(bf16[2,512,8192]{2,1,0:T(8,128)(2,1)} %all-gather.14.cloned.1.call-done, f32[128,512]{1,0:T(8,128)S(1)} %get-tuple-element.14, f32[512]{0:T(512)S(1)} %bitcast.326, f32[128]{0:T(128)S(1)} %add_rsqrt_fusion.2), kind=kOutput, calls=%fused_computation.4 | convolution fusion | flops 1074987008 | bytes 10750464 | tf_op jit(solution)/shard_map/dot_general | solution.py:137
  211.0 4.6 %all-to-all-start.6 = ((bf16[4,32,8192]{2,1,0:T(8,128)(2,1)}), bf16[4,32,8192]{2,1,0:T(8,128)(2,1)}, u32[]{:S(2)}, u32[]{:S(2)}) async-start(bf16[4,32,8192]{2,1,0:T(8,128)(2,1)} %bitcast.277), calls=%async_computation.6 | async-start | bytes 4194304 | tf_op jit(solution)/shard_map/all_to_all | solution.py:138
  215.8 25.4 %all-to-all-done.6 = bf16[4,32,8192]{2,1,0:T(8,128)(2,1)} async-done(((bf16[4,32,8192]{2,1,0:T(8,128)(2,1)}), bf16[4,32,8192]{2,1,0:T(8,128)(2,1)}, u32[]{:S(2)}, u32[]{:S(2)}) %all-to-all-start.6) | async-done | bytes 2097184 | tf_op jit(solution)/shard_map/all_to_all | solution.py:138
  247.2 17.3 %all_to_all.65 = bf16[4,32,2048]{2,1,0:T(8,128)(2,1)} all-to-all(bf16[4,32,2048]{2,1,0:T(8,128)(2,1)S(1)} %get-tuple-element.11), channel_id=1, replica_groups=mesh['dp'=4,'section'=2,'tensor'=4] {'dp'}, dimensions={0} | all-to-all | bytes 1048576 | tf_op jit(solution)/shard_map/all_to_all | solution.py:102
  264.6 33.5 %all-gather.16.cloned.1.call-done = bf16[4,128,2048]{2,1,0:T(8,128)(2,1)} async-done(((bf16[4,32,2048]{2,1,0:T(8,128)(2,1)}), bf16[4,128,2048]{2,1,0:T(8,128)(2,1)}) %all-gather.16.cloned.1.call-update) | async-done | bytes 2097168 | tf_op jit(solution)/shard_map/all_gather | solution.py:104
  298.0 3.0 fusion.164
  301.0 4.6 %all-to-all-start.9 = ((f32[4,128,8]{1,2,0:T(8,128)}), f32[4,128,8]{1,2,0:T(8,128)S(1)}, u32[]{:S(2)}, u32[]{:S(2)}) async-start(f32[4,128,8]{1,2,0:T(8,128)} %fusion.164), calls=%async_computation.9 | async-start | bytes 32768 | tf_op jit(solution)/shard_map/all_to_all | solution.py:109
  305.6 6.4 %fusion.3 = bf16[512,1280]{1,0:T(8,128)(2,1)} fusion(bf16[512,2048]{1,0:T(8,128)(2,1)S(1)} %bitcast.276, bf16[2,2048,1280]{2,1,0:T(8,128)(2,1)} %all-gather.12.cloned.1.call-done), kind=kOutput, calls=%fused_computation.14 | convolution fusion | flops 2685009920 | bytes 8650752 | tf_op jit(solution)/shard_map/dot_general | solution.py:106
  312.1 5.1 %all-to-all-start.8 = ((bf16[4,128,1280]{2,1,0:T(8,128)(2,1)}), bf16[4,128,1280]{2,1,0:T(8,128)(2,1)S(1)}, u32[]{:S(2)}, u32[]{:S(2)}) async-start(bf16[4,128,1280]{2,1,0:T(8,128)(2,1)} %bitcast.279), calls=%async_computation.8 | async-start | bytes 2621440 | tf_op jit(solution)/shard_map/all_to_all | solution.py:108
  321.3 26.6 %all-to-all-done.8 = bf16[4,128,1280]{2,1,0:T(8,128)(2,1)S(1)} async-done(((bf16[4,128,1280]{2,1,0:T(8,128)(2,1)}), bf16[4,128,1280]{2,1,0:T(8,128)(2,1)S(1)}, u32[]{:S(2)}, u32[]{:S(2)}) %all-to-all-start.8) | async-done | bytes 1310752 | tf_op jit(solution)/shard_map/all_to_all | solution.py:108
  348.1 2.5 all_gather.54
  354.8 4.7 %convolution_convert_fusion = bf16[128,8192]{1,0:T(8,128)(2,1)S(1)} fusion(bf16[2,512,8192]{2,1,0:T(8,128)(2,1)} %all-gather.14.cloned.1.call-done, f32[128,512]{1,0:T(8,128)S(1)} %get-tuple-element.8, f32[512]{0:T(512)S(1)} %bitcast.325, f32[128]{0:T(128)S(1)} %add_rsqrt_fusion), kind=kOutput, calls=%fused_computation.3 | convolution fusion | flops 1074987008 | bytes 10750464 | tf_op jit(solution)/shard_map/dot_general | solution.py:137
  359.5 28.4 %all_to_all.66 = bf16[4,32,8192]{2,1,0:T(8,128)(2,1)S(1)} all-to-all(bf16[4,32,8192]{2,1,0:T(8,128)(2,1)S(1)} %bitcast.278), channel_id=1, replica_groups=mesh['dp'=4,'section'=2,'tensor'=4] {'tensor'}, dimensions={0} | all-to-all | bytes 4194304 | tf_op jit(solution)/shard_map/all_to_all | solution.py:138
  388.5 17.5 %all_to_all.67 = bf16[8,32,2048]{2,1,0:T(8,128)(2,1)S(1)} all-to-all(bf16[8,32,2048]{2,1,0:T(8,128)(2,1)S(1)} %pad_maximum_fusion), channel_id=1, replica_groups=mesh['dp'=4,'section'=2,'tensor'=4] {'section','tensor'}, dimensions={0} | all-to-all | bytes 2097152 | tf_op jit(solution)/shard_map/all_to_all | solution.py:145
  (275 shorter events, 67.1 us)
Async XLA Ops:
  6.5 10.8 %copy-start = (bf16[256,2048]{1,0:T(8,128)(2,1)S(1)}, bf16[256,2048]{1,0:T(8,128)(2,1)}, u32[]{:S(2)}) copy-start(bf16[256,2048]{1,0:T(8,128)(2,1)} %param.11) | copy-start | bytes 3145732
  10.9 11.8 %all-to-all-start = ((s32[4,1,128]{2,1,0:T(1,128)}), s32[4,1,128]{2,1,0:T(1,128)S(1)}, u32[]{:S(2)}, u32[]{:S(2)}) async-start(s32[4,1,128]{2,1,0:T(1,128)} %bitcast.3), calls=%async_computation | async-start | bytes 4096 | tf_op jit(solution)/shard_map/all_to_all | solution.py:81
  19.9 38.2 %copy-start.8 = (f32[1,8192]{1,0:T(1,128)S(1)}, f32[1,8192]{1,0:T(1,128)}, u32[]{:S(2)}) copy-start(f32[1,8192]{1,0:T(1,128)} %param.14) | copy-start | bytes 98308
  22.7 28.2 %all-to-all-start.1 = ((bf16[4,128,1024]{2,1,0:T(8,128)(2,1)}), bf16[4,128,1024]{2,1,0:T(8,128)(2,1)S(1)}, u32[]{:S(2)}, u32[]{:S(2)}) async-start(bf16[4,128,1024]{2,1,0:T(8,128)(2,1)} %bitcast.6), calls=%async_computation.1 | async-start | bytes 2097152 | tf_op jit(solution)/shard_map/all_to_all | solution.py:78
  54.4 12.9 %all-to-all-start.2 = ((bf16[8,32,1024]{2,1,0:T(8,128)(2,1)}), bf16[8,32,1024]{2,1,0:T(8,128)(2,1)S(1)}, u32[]{:S(2)}, u32[]{:S(2)}) async-start(bf16[8,32,1024]{2,1,0:T(8,128)(2,1)} %bitcast.8), calls=%async_computation.2 | async-start | bytes 1048576 | tf_op jit(solution)/shard_map/all_to_all | solution.py:91
  58.1 61.1 %all-gather.10.cloned.1.call-start = ((), (), s32[]{:S(2)}) async-start(), calls=%async_computation.12 | async-start | bytes 2621440 | tf_op jit(solution)/shard_map/all_gather | solution.py:104
  86.3 57.1 %all-gather.12.cloned.1.call-start = ((), (), s32[]{:S(2)}) async-start(), calls=%async_computation.13 | async-start | bytes 15728640 | tf_op jit(solution)/shard_map/all_gather | solution.py:57
  87.1 9.1 %copy-start.32 = (f32[1,512]{1,0:T(1,128)S(1)}, f32[1,512]{1,0:T(1,128)}, u32[]{:S(2)}) copy-start(f32[1,512]{1,0:T(1,128)} %param.20) | copy-start | bytes 6148
  87.1 10.9 %copy-start.6 = (bf16[1,8192,8]{1,2,0:T(8,128)(2,1)S(1)}, bf16[1,8192,8]{1,2,0:T(8,128)(2,1)}, u32[]{:S(2)}) copy-start(bf16[1,8192,8]{1,2,0:T(8,128)(2,1)} %param.16) | copy-start | bytes 393220
  87.1 117.8 %all-gather.14.cloned.1.call-start = ((), (), s32[]{:S(2)}) async-start(), calls=%async_computation.14 | async-start | bytes 25165824 | tf_op jit(solution)/shard_map/all_gather | solution.py:57
  102.4 54.5 %copy-start.19 = (f32[64]{0:T(128)}, f32[64]{0:T(128)S(1)}, u32[]{:S(2)}) copy-start(f32[64]{0:T(128)S(1)} %get-tuple-element.63) | copy-start | bytes 772
  102.4 56.3 %copy-start.17 = (f32[64]{0:T(128)}, f32[64]{0:T(128)S(1)}, u32[]{:S(2)}) copy-start(f32[64]{0:T(128)S(1)} %get-tuple-element.64) | copy-start | bytes 772
  103.7 46.9 %copy-start.27 = (f32[64]{0:T(128)}, f32[64]{0:T(128)S(1)}, u32[]{:S(2)}) copy-start(f32[64]{0:T(128)S(1)} %get-tuple-element.67) | copy-start | bytes 772
  103.7 52.8 %copy-start.25 = (f32[64]{0:T(128)}, f32[64]{0:T(128)S(1)}, u32[]{:S(2)}) copy-start(f32[64]{0:T(128)S(1)} %get-tuple-element.70) | copy-start | bytes 772
  103.7 55.0 %copy-start.21 = (f32[64]{0:T(128)}, f32[64]{0:T(128)S(1)}, u32[]{:S(2)}) copy-start(f32[64]{0:T(128)S(1)} %get-tuple-element.68) | copy-start | bytes 772
  103.7 55.0 %copy-start.23 = (f32[64]{0:T(128)}, f32[64]{0:T(128)S(1)}, u32[]{:S(2)}) copy-start(f32[64]{0:T(128)S(1)} %get-tuple-element.69) | copy-start | bytes 772
  105.7 86.9 %copy-start.15 = (pred[64,64]{1,0:T(8,128)(4,1)}, pred[64,64]{1,0:T(8,128)(4,1)S(1)}, u32[]{:S(2)}) copy-start(pred[64,64]{1,0:T(8,128)(4,1)S(1)} %fusion.173) | copy-start | bytes 12292
  122.0 10.2 %all-to-all-start.5 = ((f32[4,128,8]{1,2,0:T(8,128)}), f32[4,128,8]{1,2,0:T(8,128)S(1)}, u32[]{:S(2)}, u32[]{:S(2)}) async-start(f32[4,128,8]{1,2,0:T(8,128)} %fusion.166), calls=%async_computation.5 | async-start | bytes 32768 | tf_op jit(solution)/shard_map/all_to_all | solution.py:109
  126.6 28.8 %copy-start.30 = (f32[64]{0:T(128)}, f32[64]{0:T(128)S(1)}, u32[]{:S(2)}) copy-start(f32[64]{0:T(128)S(1)} %compare_convert_fusion.2) | copy-start | bytes 772
  150.5 36.8 %all-to-all-start.4 = ((bf16[4,128,1280]{2,1,0:T(8,128)(2,1)}), bf16[4,128,1280]{2,1,0:T(8,128)(2,1)}, u32[]{:S(2)}, u32[]{:S(2)}) async-start(bf16[4,128,1280]{2,1,0:T(8,128)(2,1)} %bitcast.280), calls=%async_computation.4 | async-start | bytes 2621440 | tf_op jit(solution)/shard_map/all_to_all | solution.py:108
  211.0 30.1 %all-to-all-start.6 = ((bf16[4,32,8192]{2,1,0:T(8,128)(2,1)}), bf16[4,32,8192]{2,1,0:T(8,128)(2,1)}, u32[]{:S(2)}, u32[]{:S(2)}) async-start(bf16[4,32,8192]{2,1,0:T(8,128)(2,1)} %bitcast.277), calls=%async_computation.6 | async-start | bytes 4194304 | tf_op jit(solution)/shard_map/all_to_all | solution.py:138
  215.7 82.4 %all-gather.16.cloned.1.call-start = ((), (), s32[]{:S(2)}) async-start(), calls=%async_computation.15 | async-start | bytes 2621440 | tf_op jit(solution)/shard_map/all_gather | solution.py:104
  301.0 11.1 %all-to-all-start.9 = ((f32[4,128,8]{1,2,0:T(8,128)}), f32[4,128,8]{1,2,0:T(8,128)S(1)}, u32[]{:S(2)}, u32[]{:S(2)}) async-start(f32[4,128,8]{1,2,0:T(8,128)} %fusion.164), calls=%async_computation.9 | async-start | bytes 32768 | tf_op jit(solution)/shard_map/all_to_all | solution.py:109
  312.1 7.8 %copy-start.31 = (f32[64]{0:T(128)S(1)}, f32[64]{0:T(128)}, u32[]{:S(2)}) copy-start(f32[64]{0:T(128)} %copy-done.30) | copy-start | bytes 772
  312.1 8.3 %copy-start.26 = (f32[64]{0:T(128)S(1)}, f32[64]{0:T(128)}, u32[]{:S(2)}) copy-start(f32[64]{0:T(128)} %copy-done.25) | copy-start | bytes 772
  312.1 8.8 %copy-start.20 = (f32[64]{0:T(128)S(1)}, f32[64]{0:T(128)}, u32[]{:S(2)}) copy-start(f32[64]{0:T(128)} %copy-done.19) | copy-start | bytes 772
  312.1 9.0 %copy-start.18 = (f32[64]{0:T(128)S(1)}, f32[64]{0:T(128)}, u32[]{:S(2)}) copy-start(f32[64]{0:T(128)} %copy-done.17) | copy-start | bytes 772
  312.1 9.0 %copy-start.22 = (f32[64]{0:T(128)S(1)}, f32[64]{0:T(128)}, u32[]{:S(2)}) copy-start(f32[64]{0:T(128)} %copy-done.21) | copy-start | bytes 772
  312.1 9.0 %copy-start.24 = (f32[64]{0:T(128)S(1)}, f32[64]{0:T(128)}, u32[]{:S(2)}) copy-start(f32[64]{0:T(128)} %copy-done.23) | copy-start | bytes 772
  312.1 35.7 %all-to-all-start.8 = ((bf16[4,128,1280]{2,1,0:T(8,128)(2,1)}), bf16[4,128,1280]{2,1,0:T(8,128)(2,1)S(1)}, u32[]{:S(2)}, u32[]{:S(2)}) async-start(bf16[4,128,1280]{2,1,0:T(8,128)(2,1)} %bitcast.279), calls=%async_computation.8 | async-start | bytes 2621440 | tf_op jit(solution)/shard_map/all_to_all | solution.py:108
  321.2 30.4 %copy-start.16 = (pred[64,64]{1,0:T(8,128)(4,1)S(1)}, pred[64,64]{1,0:T(8,128)(4,1)}, u32[]{:S(2)}) copy-start(pred[64,64]{1,0:T(8,128)(4,1)} %copy-done.15) | copy-start | bytes 12292
  388.4 18.6 %copy-start.1 = (bf16[256,2048]{1,0:T(8,128)(2,1)S(1)}, bf16[256,2048]{1,0:T(8,128)(2,1)}, u32[]{:S(2)}) copy-start(bf16[256,2048]{1,0:T(8,128)(2,1)} %param.11) | copy-start | bytes 3145732
  (20 other events, 78.5 us)
Sparse Core Ops, SparseCore 0:
  86.4 32.6 all-gather.9
  120.7 22.6 all-gather.11
  144.9 31.2 all-gather.13
  264.7 33.2 all-gather.15
where the time goes:
time: 415 us; the launch traced here: 414 us
  waiting for transfers between devices  172 us (41%)
  blocking collectives  101 us (24%)
  matrix products  42.6 us (10%)
  starting transfers between devices  37.5 us (9%)
  local copies, waits for them, and re-layouts  25.3 us (6%)
  other arithmetic  19.1 us (5%)
  between operations  15.9 us (4%)
    all_to_all x2, waiting for transfers between devices, per_device(): lax.all_to_all(proj.reshape(groups, half, -1), 'dp', 0, 0, tiled=True)  54.5 us
    all_gather x2, waiting for transfers between devices, per_device(): full_u = lax.all_gather(u, 'tensor', axis=1, tiled=True)  45.6 us
    all_to_all x2, blocking collectives, per_device(): u = lax.all_to_all(u, 'dp', 0, 0, tiled=True)  35.7 us
    all_to_all x1, blocking collectives, per_device(): lax.all_to_all(partial_value.reshape(width, few, feats), 'tensor', 0, 0,...  28.4 us
    all_to_all x1, waiting for transfers between devices, per_device(): lax.all_to_all(partial_value.reshape(width, few, feats), 'tensor', 0, 0,...  25.4 us
    all_to_all x1, waiting for transfers between devices, per_device(): lax.all_to_all(outbox.reshape(groups, capacity, part), 'dp', split_axis=0...  24.7 us
    all_to_all x1, blocking collectives, per_device(): outs = lax.all_to_all(outs, ('section', 'tensor'), 0, 0, tiled=True)  17.5 us
    dot_general x2, matrix products, per_device(): proj = jnp.dot(full_u, w_in[layer], preferred_element_type=f32).astype(bf16)  13.6 us
  transfers between devices with their start and end apart: 12, of which 10 were waited for; matrix products, arithmetic and copies ran while one was open for 13% of the time, Pallas kernels for 0%

commit v1 on v0

--- a/solution.py
+++ b/solution.py
@@ -101,7 +101,24 @@
         u = u.reshape(few, groups, depth).transpose(1, 0, 2)
         u = lax.all_to_all(u, "dp", 0, 0, tiled=True)
         step_w = lax.dynamic_slice_in_dim(w_step[layer], dp_idx * depth, depth, axis=0)
-        full_u = lax.all_gather(u, "tensor", axis=1, tiled=True)
+
+        def proceed_run(local_x):
+            size_here = lax.axis_size("tensor")
+            u1 = range(1, size_here)
+            low = map(lambda kk: (kk - 1, kk), u1)
+            frame_out = list(low)
+            x_now = local_x
+            plain = frame_out + [(size_here - 1, 0)]
+            fields = [x_now]
+            for _ in range(size_here - 1):
+                x_now = lax.ppermute(x_now, perm=plain, axis_name="tensor")
+                fields += [x_now]
+            current_block = jnp.concatenate([*reversed(fields)], 1)
+            block_next = lax.axis_index("tensor")
+            f_now = jnp.roll(current_block, (block_next + 1) * x_now.shape[1], 1)
+            return f_now
+
+        full_u = proceed_run(u)
         full_u = full_u.reshape(groups * half, depth)
         proj = jnp.dot(full_u, w_in[layer], preferred_element_type=f32).astype(bf16)
         pre = jnp.dot(full_u, step_w, preferred_element_type=f32)

time: 415 us -> 423 us (1.019)
  blocking collectives: 101 us -> 83.5 us
  waiting for transfers between devices: 172 us -> 189 us
  other arithmetic: 19.1 us -> 28 us
  matrix products: 42.6 us -> 38.2 us
    ppermute x0 -> x6, waiting for transfers between devices: none -> 64.7 us  [proceed_run(): x_now = lax.ppermute(x_now, perm=plain, axis_name='tensor')]
    all_gather x2 -> x0, waiting for transfers between devices: 45.6 us -> none  [per_device(): full_u = lax.all_gather(u, 'tensor', axis=1, tiled=True)]
    all_to_all x2 -> x1, blocking collectives: 35.7 us -> 17.4 us  [per_device(): u = lax.all_to_all(u, 'dp', 0, 0, tiled=True)]
    all_to_all x0 -> x1, waiting for transfers between devices: none -> 10.4 us  [per_device(): u = lax.all_to_all(u, 'dp', 0, 0, tiled=True)]
    concatenate x0 -> x2, other arithmetic: none -> 9.87 us  [proceed_run(): f_now = jnp.roll(current_block, (block_next + 1) * x_now.shape[1], 1)]
    all_gather x2, waiting for transfers between devices: 7.31 us -> 0.02 us  [whole(): return lax.all_gather(param, 'section', axis=0, tiled=True)]
  transfers between devices with their start and end apart: 12 -> 17, of which waited for: 10 -> 14; matrix products, arithmetic and copies ran while one was open for 13% -> 15% of each run, Pallas kernels for 0% -> 0%
where the time goes in v1:
time: 423 us; the launch traced here: 422 us
  waiting for transfers between devices  189 us (45%)
  blocking collectives  83.5 us (20%)
  starting transfers between devices  40.1 us (9%)
  matrix products  38.2 us (9%)
  other arithmetic  28 us (7%)
  local copies, waits for them, and re-layouts  26.2 us (6%)
  between operations  16.3 us (4%)
    ppermute x6, waiting for transfers between devices, proceed_run(): x_now = lax.ppermute(x_now, perm=plain, axis_name='tensor')  64.7 us
    all_to_all x2, waiting for transfers between devices, per_device(): lax.all_to_all(proj.reshape(groups, half, -1), 'dp', 0, 0, tiled=True)  51.4 us
    all_to_all x1, blocking collectives, per_device(): lax.all_to_all(partial_value.reshape(width, few, feats), 'tensor', 0, 0,...  28.6 us
    all_to_all x1, waiting for transfers between devices, per_device(): lax.all_to_all(partial_value.reshape(width, few, feats), 'tensor', 0, 0,...  26.2 us
    all_to_all x1, waiting for transfers between devices, per_device(): lax.all_to_all(outbox.reshape(groups, capacity, part), 'dp', split_axis=0...  24.4 us
    all_to_all x1, blocking collectives, per_device(): outs = lax.all_to_all(outs, ('section', 'tensor'), 0, 0, tiled=True)  17.5 us
    all_to_all x1, blocking collectives, per_device(): u = lax.all_to_all(u, 'dp', 0, 0, tiled=True)  17.4 us
    dot_general x2, matrix products, per_device(): proj = jnp.dot(full_u, w_in[layer], preferred_element_type=f32).astype(bf16)  13.6 us
  transfers between devices with their start and end apart: 17, of which 14 were waited for; matrix products, arithmetic and copies ran while one was open for 15% of the time, Pallas kernels for 0%

profile of v1, /device:TPU:0, one launch (start us, length us, event | category | flops | bytes accessed | tf_op | source)
XLA Modules:
  0.0 421.5 jit_solution(2271183598660476261)
XLA Ops:
  11.6 6.3 %all-to-all-start = ((s32[4,1,128]{2,1,0:T(1,128)}), s32[4,1,128]{2,1,0:T(1,128)S(1)}, u32[]{:S(2)}, u32[]{:S(2)}) async-start(s32[4,1,128]{2,1,0:T(1,128)} %bitcast.3), calls=%async_computation | async-start | bytes 4096 | tf_op jit(solution)/shard_map/all_to_all | solution.py:81
  23.6 3.5 all-to-all-start.1
  27.1 24.4 %all-to-all-done.1 = bf16[4,128,1024]{2,1,0:T(8,128)(2,1)S(1)} async-done(((bf16[4,128,1024]{2,1,0:T(8,128)(2,1)}), bf16[4,128,1024]{2,1,0:T(8,128)(2,1)S(1)}, u32[]{:S(2)}, u32[]{:S(2)}) %all-to-all-start.1) | async-done | bytes 1048608 | tf_op jit(solution)/shard_map/all_to_all | solution.py:78
  51.5 3.4 scatter_custom_fusion.2
  55.0 3.7 all-to-all-start.2
  63.8 4.0 all-to-all-done.2
  69.2 3.5 all-to-all-start.3
  77.6 10.4 %all-to-all-done.3 = bf16[4,32,2048]{2,1,0:T(8,128)(2,1)S(1)} async-done(((bf16[4,32,2048]{2,1,0:T(8,128)(2,1)}), bf16[4,32,2048]{2,1,0:T(8,128)(2,1)S(1)}, u32[]{:S(2)}, u32[]{:S(2)}) %all-to-all-start.3) | async-done | bytes 524320 | tf_op jit(solution)/shard_map/all_to_all | solution.py:102
  95.8 6.5 %collective-permute-done = bf16[4,32,2048]{2,1,0:T(8,128)(2,1)S(1)} collective-permute-done((bf16[4,32,2048]{2,1,0:T(8,128)(2,1)S(1)}, bf16[4,32,2048]{2,1,0:T(8,128)(2,1)S(1)}, u32[]{:S(2)}, u32[]{:S(2)}) %collective-permute-start) | collective-permute-done | bytes 524320 | tf_op jit(solution)/shard_map/ppermute | solution.py:114
  104.9 10.8 %collective-permute-done.1 = bf16[4,32,2048]{2,1,0:T(8,128)(2,1)S(1)} collective-permute-done((bf16[4,32,2048]{2,1,0:T(8,128)(2,1)S(1)}, bf16[4,32,2048]{2,1,0:T(8,128)(2,1)S(1)}, u32[]{:S(2)}, u32[]{:S(2)}) %collective-permute-start.1) | collective-permute-done | bytes 524320 | tf_op jit(solution)/shard_map/ppermute | solution.py:114
  117.9 10.4 %collective-permute-done.2 = bf16[4,32,2048]{2,1,0:T(8,128)(2,1)} collective-permute-done((bf16[4,32,2048]{2,1,0:T(8,128)(2,1)S(1)}, bf16[4,32,2048]{2,1,0:T(8,128)(2,1)}, u32[]{:S(2)}, u32[]{:S(2)}) %collective-permute-start.2) | collective-permute-done | bytes 524320 | tf_op jit(solution)/shard_map/ppermute | solution.py:114
  128.4 5.2 %fusion.14 = bf16[4,128,2048]{2,1,0:T(8,128)(2,1)S(1)} fusion(s32[]{:T(128)S(6)} %select_n.132, bf16[4,32,2048]{2,1,0:T(8,128)(2,1)} %collective-permute-done.2, bf16[4,32,2048]{2,1,0:T(8,128)(2,1)S(1)} %collective-permute-done.1, bf16[4,32,2048]{2,1,0:T(8,128)(2,1)S(1)} %collective-permute-done, bf16[4,32,2048]{2,1,0:T(8,128)(2,1)S(1)} %all-to-all-done.3), kind=kLoop, calls=%fused_computation.41 | loop fusion | flops 16777216 | bytes 4194308 | tf_op jit(solution)/shard_map/jit(_roll_dynamic)/concatenate | solution.py:118
  136.2 3.3 all-to-all-start.5
  141.4 3.6 all-to-all-done.5
  148.2 7.2 %fusion.2 = bf16[512,1280]{1,0:T(8,128)(2,1)} fusion(bf16[512,2048]{1,0:T(8,128)(2,1)} %bitcast.269, bf16[2,2048,1280]{2,1,0:T(8,128)(2,1)} %all-gather.8.cloned.1.call-done), kind=kOutput, calls=%fused_computation.29 | convolution fusion | flops 2685009920 | bytes 8650752 | tf_op jit(solution)/shard_map/dot_general | solution.py:123
  155.3 3.5 all-to-all-start.4
  163.3 27.5 %all-to-all-done.4 = bf16[4,128,1280]{2,1,0:T(8,128)(2,1)S(1)} async-done(((bf16[4,128,1280]{2,1,0:T(8,128)(2,1)}), bf16[4,128,1280]{2,1,0:T(8,128)(2,1)S(1)}, u32[]{:S(2)}, u32[]{:S(2)}) %all-to-all-start.4) | async-done | bytes 1310752 | tf_op jit(solution)/shard_map/all_to_all | solution.py:125
  205.6 6.0 %convolution_convert_fusion.1 = bf16[128,8192]{1,0:T(8,128)(2,1)} fusion(bf16[2,512,8192]{2,1,0:T(8,128)(2,1)} %all-gather.10.cloned.1.call-done, f32[128,512]{1,0:T(8,128)S(1)} %get-tuple-element.15, f32[512]{0:T(512)} %bitcast.323, f32[128]{0:T(128)S(1)} %add_rsqrt_fusion.2), kind=kOutput, calls=%fused_computation.4 | convolution fusion | flops 1074987008 | bytes 10750464 | tf_op jit(solution)/shard_map/dot_general | solution.py:154
  211.6 4.6 %all-to-all-start.6 = ((bf16[4,32,8192]{2,1,0:T(8,128)(2,1)}), bf16[4,32,8192]{2,1,0:T(8,128)(2,1)}, u32[]{:S(2)}, u32[]{:S(2)}) async-start(bf16[4,32,8192]{2,1,0:T(8,128)(2,1)} %bitcast.274), calls=%async_computation.6 | async-start | bytes 4194304 | tf_op jit(solution)/shard_map/all_to_all | solution.py:155
  216.2 26.2 %all-to-all-done.6 = bf16[4,32,8192]{2,1,0:T(8,128)(2,1)} async-done(((bf16[4,32,8192]{2,1,0:T(8,128)(2,1)}), bf16[4,32,8192]{2,1,0:T(8,128)(2,1)}, u32[]{:S(2)}, u32[]{:S(2)}) %all-to-all-start.6) | async-done | bytes 2097184 | tf_op jit(solution)/shard_map/all_to_all | solution.py:155
  249.3 17.4 %all_to_all.64 = bf16[4,32,2048]{2,1,0:T(8,128)(2,1)S(1)} all-to-all(bf16[4,32,2048]{2,1,0:T(8,128)(2,1)S(1)} %get-tuple-element.12), channel_id=1, replica_groups=mesh['dp'=4,'section'=2,'tensor'=4] {'dp'}, dimensions={0} | all-to-all | bytes 1048576 | tf_op jit(solution)/shard_map/all_to_all | solution.py:102
  268.1 12.4 %collective-permute-done.3 = bf16[4,32,2048]{2,1,0:T(8,128)(2,1)S(1)} collective-permute-done((bf16[4,32,2048]{2,1,0:T(8,128)(2,1)S(1)}, bf16[4,32,2048]{2,1,0:T(8,128)(2,1)S(1)}, u32[]{:S(2)}, u32[]{:S(2)}) %collective-permute-start.3) | collective-permute-done | bytes 524320 | tf_op jit(solution)/shard_map/ppermute | solution.py:114
  281.1 12.5 %collective-permute-done.4 = bf16[4,32,2048]{2,1,0:T(8,128)(2,1)S(1)} collective-permute-done((bf16[4,32,2048]{2,1,0:T(8,128)(2,1)S(1)}, bf16[4,32,2048]{2,1,0:T(8,128)(2,1)S(1)}, u32[]{:S(2)}, u32[]{:S(2)}) %collective-permute-start.4) | collective-permute-done | bytes 524320 | tf_op jit(solution)/shard_map/ppermute | solution.py:114
  293.6 12.1 %collective-permute-done.5 = bf16[4,32,2048]{2,1,0:T(8,128)(2,1)S(1)} collective-permute-done((bf16[4,32,2048]{2,1,0:T(8,128)(2,1)S(1)}, bf16[4,32,2048]{2,1,0:T(8,128)(2,1)S(1)}, u32[]{:S(2)}, u32[]{:S(2)}) %collective-permute-start.5) | collective-permute-done | bytes 524320 | tf_op jit(solution)/shard_map/ppermute | solution.py:114
  305.7 4.6 %fusion.7 = bf16[4,128,2048]{2,1,0:T(8,128)(2,1)S(1)} fusion(s32[]{:T(128)S(6)} %select_n.132, bf16[4,32,2048]{2,1,0:T(8,128)(2,1)S(1)} %collective-permute-done.5, bf16[4,32,2048]{2,1,0:T(8,128)(2,1)S(1)} %collective-permute-done.4, bf16[4,32,2048]{2,1,0:T(8,128)(2,1)S(1)} %collective-permute-done.3, bf16[4,32,2048]{2,1,0:T(8,128)(2,1)S(1)} %all_to_all.64), kind=kLoop, calls=%fused_computation.34 | loop fusion | flops 16777216 | bytes 4194308 | tf_op jit(solution)/shard_map/jit(_roll_dynamic)/concatenate | solution.py:118
  312.4 3.7 all-to-all-start.9
  316.1 6.4 %fusion.3 = bf16[512,1280]{1,0:T(8,128)(2,1)} fusion(bf16[512,2048]{1,0:T(8,128)(2,1)S(1)} %bitcast.270, bf16[2,2048,1280]{2,1,0:T(8,128)(2,1)} %all-gather.8.cloned.1.call-done), kind=kOutput, calls=%fused_computation.30 | convolution fusion | flops 2685009920 | bytes 8650752 | tf_op jit(solution)/shard_map/dot_general | solution.py:123
  322.6 5.2 %all-to-all-start.8 = ((bf16[4,128,1280]{2,1,0:T(8,128)(2,1)}), bf16[4,128,1280]{2,1,0:T(8,128)(2,1)S(1)}, u32[]{:S(2)}, u32[]{:S(2)}) async-start(bf16[4,128,1280]{2,1,0:T(8,128)(2,1)} %bitcast.276), calls=%async_computation.8 | async-start | bytes 2621440 | tf_op jit(solution)/shard_map/all_to_all | solution.py:125
  331.8 23.8 %all-to-all-done.8 = bf16[4,128,1280]{2,1,0:T(8,128)(2,1)S(1)} async-done(((bf16[4,128,1280]{2,1,0:T(8,128)(2,1)}), bf16[4,128,1280]{2,1,0:T(8,128)(2,1)S(1)}, u32[]{:S(2)}, u32[]{:S(2)}) %all-to-all-start.8) | async-done | bytes 1310752 | tf_op jit(solution)/shard_map/all_to_all | solution.py:125
  362.4 4.7 %convolution_convert_fusion = bf16[128,8192]{1,0:T(8,128)(2,1)S(1)} fusion(bf16[2,512,8192]{2,1,0:T(8,128)(2,1)} %all-gather.10.cloned.1.call-done, f32[128,512]{1,0:T(8,128)S(1)} %get-tuple-element.9, f32[512]{0:T(512)S(1)} %bitcast.322, f32[128]{0:T(128)S(1)} %add_rsqrt_fusion), kind=kOutput, calls=%fused_computation.3 | convolution fusion | flops 1074987008 | bytes 10750464 | tf_op jit(solution)/shard_map/dot_general | solution.py:154
  367.1 28.6 %all_to_all.65 = bf16[4,32,8192]{2,1,0:T(8,128)(2,1)S(1)} all-to-all(bf16[4,32,8192]{2,1,0:T(8,128)(2,1)S(1)} %bitcast.275), channel_id=1, replica_groups=mesh['dp'=4,'section'=2,'tensor'=4] {'tensor'}, dimensions={0} | all-to-all | bytes 4194304 | tf_op jit(solution)/shard_map/all_to_all | solution.py:155
  396.2 17.5 %all_to_all.66 = bf16[8,32,2048]{2,1,0:T(8,128)(2,1)S(1)} all-to-all(bf16[8,32,2048]{2,1,0:T(8,128)(2,1)S(1)} %pad_maximum_fusion), channel_id=1, replica_groups=mesh['dp'=4,'section'=2,'tensor'=4] {'section','tensor'}, dimensions={0} | all-to-all | bytes 2097152 | tf_op jit(solution)/shard_map/all_to_all | solution.py:162
  (284 shorter events, 82.0 us)
Async XLA Ops:
  6.5 141.6 %all-gather.8.cloned.1.call-start = ((), (), s32[]{:S(2)}) async-start(), calls=%async_computation.12 | async-start | bytes 15728640 | tf_op jit(solution)/shard_map/all_gather | solution.py:57
  7.3 198.3 %all-gather.10.cloned.1.call-start = ((), (), s32[]{:S(2)}) async-start(), calls=%async_computation.13 | async-start | bytes 25165824 | tf_op jit(solution)/shard_map/all_gather | solution.py:57
  8.0 50.7 %copy-start.6 = (f32[1,8192]{1,0:T(1,128)S(1)}, f32[1,8192]{1,0:T(1,128)}, u32[]{:S(2)}) copy-start(f32[1,8192]{1,0:T(1,128)} %param.16) | copy-start | bytes 98308
  8.0 53.6 %copy-start.4 = (bf16[1,8192,8]{1,2,0:T(8,128)(2,1)S(1)}, bf16[1,8192,8]{1,2,0:T(8,128)(2,1)}, u32[]{:S(2)}) copy-start(bf16[1,8192,8]{1,2,0:T(8,128)(2,1)} %param.18) | copy-start | bytes 393220
  11.6 11.9 %all-to-all-start = ((s32[4,1,128]{2,1,0:T(1,128)}), s32[4,1,128]{2,1,0:T(1,128)S(1)}, u32[]{:S(2)}, u32[]{:S(2)}) async-start(s32[4,1,128]{2,1,0:T(1,128)} %bitcast.3), calls=%async_computation | async-start | bytes 4096 | tf_op jit(solution)/shard_map/all_to_all | solution.py:81
  23.6 28.0 %all-to-all-start.1 = ((bf16[4,128,1024]{2,1,0:T(8,128)(2,1)}), bf16[4,128,1024]{2,1,0:T(8,128)(2,1)S(1)}, u32[]{:S(2)}, u32[]{:S(2)}) async-start(bf16[4,128,1024]{2,1,0:T(8,128)(2,1)} %bitcast.6), calls=%async_computation.1 | async-start | bytes 2097152 | tf_op jit(solution)/shard_map/all_to_all | solution.py:78
  55.0 12.9 %all-to-all-start.2 = ((bf16[8,32,1024]{2,1,0:T(8,128)(2,1)}), bf16[8,32,1024]{2,1,0:T(8,128)(2,1)S(1)}, u32[]{:S(2)}, u32[]{:S(2)}) async-start(bf16[8,32,1024]{2,1,0:T(8,128)(2,1)} %bitcast.8), calls=%async_computation.2 | async-start | bytes 1048576 | tf_op jit(solution)/shard_map/all_to_all | solution.py:91
  60.9 42.1 %copy-start.39 = (f32[1,8]{1,0:T(1,128)S(1)}, f32[1,8]{1,0:T(1,128)}, u32[]{:S(2)}) copy-start(f32[1,8]{1,0:T(1,128)} %param.21) | copy-start | bytes 100
  69.2 18.8 %all-to-all-start.3 = ((bf16[4,32,2048]{2,1,0:T(8,128)(2,1)}), bf16[4,32,2048]{2,1,0:T(8,128)(2,1)S(1)}, u32[]{:S(2)}, u32[]{:S(2)}) async-start(bf16[4,32,2048]{2,1,0:T(8,128)(2,1)} %fusion.42), calls=%async_computation.3 | async-start | bytes 1048576 | tf_op jit(solution)/shard_map/all_to_all | solution.py:102
  88.0 14.3 %collective-permute-start = (bf16[4,32,2048]{2,1,0:T(8,128)(2,1)S(1)}, bf16[4,32,2048]{2,1,0:T(8,128)(2,1)S(1)}, u32[]{:S(2)}, u32[]{:S(2)}) collective-permute-start(bf16[4,32,2048]{2,1,0:T(8,128)(2,1)S(1)} %all-to-all-done.3), channel_id=1, source_target_pairs={{0,1},{1,2},{2,3},{3,0},{4,5},{5,6},{6,7},{7,4},{8,9},{9,10},{10,1... | collective-permute-start | bytes 1572872 | tf_op jit(solution)/shard_map/ppermute | solution.py:114
  95.2 63.7 %copy-start.25 = (f32[64]{0:T(128)}, f32[64]{0:T(128)S(1)}, u32[]{:S(2)}) copy-start(f32[64]{0:T(128)S(1)} %get-tuple-element.71) | copy-start | bytes 772
  95.2 64.5 %copy-start.23 = (f32[64]{0:T(128)}, f32[64]{0:T(128)S(1)}, u32[]{:S(2)}) copy-start(f32[64]{0:T(128)S(1)} %get-tuple-element.68) | copy-start | bytes 772
  95.2 67.4 %copy-start.19 = (f32[64]{0:T(128)}, f32[64]{0:T(128)S(1)}, u32[]{:S(2)}) copy-start(f32[64]{0:T(128)S(1)} %get-tuple-element.69) | copy-start | bytes 772
  95.2 67.3 %copy-start.21 = (f32[64]{0:T(128)}, f32[64]{0:T(128)S(1)}, u32[]{:S(2)}) copy-start(f32[64]{0:T(128)S(1)} %get-tuple-element.70) | copy-start | bytes 772
  102.3 13.4 %collective-permute-start.1 = (bf16[4,32,2048]{2,1,0:T(8,128)(2,1)S(1)}, bf16[4,32,2048]{2,1,0:T(8,128)(2,1)S(1)}, u32[]{:S(2)}, u32[]{:S(2)}) collective-permute-start(bf16[4,32,2048]{2,1,0:T(8,128)(2,1)S(1)} %collective-permute-done), channel_id=1, source_target_pairs={{0,1},{1,2},{2,3},{3,0},{4,5},{5,6},{6,7},{7,4},{8,9},{9,10},{10,1... | collective-permute-start | bytes 1572872 | tf_op jit(solution)/shard_map/ppermute | solution.py:114
  102.9 52.4 %copy-start.17 = (f32[64]{0:T(128)}, f32[64]{0:T(128)S(1)}, u32[]{:S(2)}) copy-start(f32[64]{0:T(128)S(1)} %get-tuple-element.64) | copy-start | bytes 772
  102.9 59.6 %copy-start.15 = (f32[64]{0:T(128)}, f32[64]{0:T(128)S(1)}, u32[]{:S(2)}) copy-start(f32[64]{0:T(128)S(1)} %get-tuple-element.65) | copy-start | bytes 772
  104.9 89.4 %copy-start.11 = (pred[64,64]{1,0:T(8,128)(4,1)}, pred[64,64]{1,0:T(8,128)(4,1)S(1)}, u32[]{:S(2)}) copy-start(pred[64,64]{1,0:T(8,128)(4,1)S(1)} %fusion.187) | copy-start | bytes 12292
  104.9 91.0 %copy-start.9 = (pred[64,64]{1,0:T(8,128)(4,1)}, pred[64,64]{1,0:T(8,128)(4,1)S(1)}, u32[]{:S(2)}) copy-start(pred[64,64]{1,0:T(8,128)(4,1)S(1)} %fusion.186) | copy-start | bytes 12292
  115.7 12.7 %collective-permute-start.2 = (bf16[4,32,2048]{2,1,0:T(8,128)(2,1)S(1)}, bf16[4,32,2048]{2,1,0:T(8,128)(2,1)}, u32[]{:S(2)}, u32[]{:S(2)}) collective-permute-start(bf16[4,32,2048]{2,1,0:T(8,128)(2,1)S(1)} %collective-permute-done.1), channel_id=1, source_target_pairs={{0,1},{1,2},{2,3},{3,0},{4,5},{5,6},{6,7},{7,4},{8,9},{9,10},{10,1... | collective-permute-start | bytes 1572872 | tf_op jit(solution)/shard_map/ppermute | solution.py:114
  116.3 80.0 %copy-start.8 = (f32[8]{0:T(128)}, f32[8]{0:T(128)S(1)}, u32[]{:S(2)}) copy-start(f32[8]{0:T(128)S(1)} %get-tuple-element.53) | copy-start | bytes 100
  136.2 8.8 %all-to-all-start.5 = ((f32[4,128,8]{1,2,0:T(8,128)}), f32[4,128,8]{1,2,0:T(8,128)S(1)}, u32[]{:S(2)}, u32[]{:S(2)}) async-start(f32[4,128,8]{1,2,0:T(8,128)} %fusion.180), calls=%async_computation.5 | async-start | bytes 32768 | tf_op jit(solution)/shard_map/all_to_all | solution.py:126
  155.3 35.5 %all-to-all-start.4 = ((bf16[4,128,1280]{2,1,0:T(8,128)(2,1)}), bf16[4,128,1280]{2,1,0:T(8,128)(2,1)S(1)}, u32[]{:S(2)}, u32[]{:S(2)}) async-start(bf16[4,128,1280]{2,1,0:T(8,128)(2,1)} %bitcast.277), calls=%async_computation.4 | async-start | bytes 2621440 | tf_op jit(solution)/shard_map/all_to_all | solution.py:125
  163.3 32.7 %copy-start.28 = (f32[8,64]{1,0:T(8,128)S(1)}, f32[8,64]{1,0:T(8,128)}, u32[]{:S(2)}) copy-start(f32[8,64]{1,0:T(8,128)} %get-tuple-element.44) | copy-start | bytes 6148
  211.6 30.9 %all-to-all-start.6 = ((bf16[4,32,8192]{2,1,0:T(8,128)(2,1)}), bf16[4,32,8192]{2,1,0:T(8,128)(2,1)}, u32[]{:S(2)}, u32[]{:S(2)}) async-start(bf16[4,32,8192]{2,1,0:T(8,128)(2,1)} %bitcast.274), calls=%async_computation.6 | async-start | bytes 4194304 | tf_op jit(solution)/shard_map/all_to_all | solution.py:155
  266.7 13.9 %collective-permute-start.3 = (bf16[4,32,2048]{2,1,0:T(8,128)(2,1)S(1)}, bf16[4,32,2048]{2,1,0:T(8,128)(2,1)S(1)}, u32[]{:S(2)}, u32[]{:S(2)}) collective-permute-start(bf16[4,32,2048]{2,1,0:T(8,128)(2,1)S(1)} %all_to_all.64), channel_id=1, source_target_pairs={{0,1},{1,2},{2,3},{3,0},{4,5},{5,6},{6,7},{7,4},{8,9},{9,10},{10,1... | collective-permute-start | bytes 1572872 | tf_op jit(solution)/shard_map/ppermute | solution.py:114
  280.6 13.0 %collective-permute-start.4 = (bf16[4,32,2048]{2,1,0:T(8,128)(2,1)S(1)}, bf16[4,32,2048]{2,1,0:T(8,128)(2,1)S(1)}, u32[]{:S(2)}, u32[]{:S(2)}) collective-permute-start(bf16[4,32,2048]{2,1,0:T(8,128)(2,1)S(1)} %collective-permute-done.3), channel_id=1, source_target_pairs={{0,1},{1,2},{2,3},{3,0},{4,5},{5,6},{6,7},{7,4},{8,9},{9,10},{10,1... | collective-permute-start | bytes 1572872 | tf_op jit(solution)/shard_map/ppermute | solution.py:114
  293.6 12.2 %collective-permute-start.5 = (bf16[4,32,2048]{2,1,0:T(8,128)(2,1)S(1)}, bf16[4,32,2048]{2,1,0:T(8,128)(2,1)S(1)}, u32[]{:S(2)}, u32[]{:S(2)}) collective-permute-start(bf16[4,32,2048]{2,1,0:T(8,128)(2,1)S(1)} %collective-permute-done.4), channel_id=1, source_target_pairs={{0,1},{1,2},{2,3},{3,0},{4,5},{5,6},{6,7},{7,4},{8,9},{9,10},{10,1... | collective-permute-start | bytes 1572872 | tf_op jit(solution)/shard_map/ppermute | solution.py:114
  312.4 10.2 %all-to-all-start.9 = ((f32[4,128,8]{1,2,0:T(8,128)}), f32[4,128,8]{1,2,0:T(8,128)S(1)}, u32[]{:S(2)}, u32[]{:S(2)}) async-start(f32[4,128,8]{1,2,0:T(8,128)} %fusion.178), calls=%async_computation.9 | async-start | bytes 32768 | tf_op jit(solution)/shard_map/all_to_all | solution.py:126
  322.6 36.3 %copy-start.12 = (pred[64,64]{1,0:T(8,128)(4,1)S(1)}, pred[64,64]{1,0:T(8,128)(4,1)}, u32[]{:S(2)}) copy-start(pred[64,64]{1,0:T(8,128)(4,1)} %copy-done.11) | copy-start | bytes 12292
  322.6 36.6 %copy-start.7 = (f32[8]{0:T(128)S(1)}, f32[8]{0:T(128)}, u32[]{:S(2)}) copy-start(f32[8]{0:T(128)} %get-tuple-element.52) | copy-start | bytes 100
  322.6 33.0 %all-to-all-start.8 = ((bf16[4,128,1280]{2,1,0:T(8,128)(2,1)}), bf16[4,128,1280]{2,1,0:T(8,128)(2,1)S(1)}, u32[]{:S(2)}, u32[]{:S(2)}) async-start(bf16[4,128,1280]{2,1,0:T(8,128)(2,1)} %bitcast.276), calls=%async_computation.8 | async-start | bytes 2621440 | tf_op jit(solution)/shard_map/all_to_all | solution.py:125
  (25 other events, 375.9 us)
Sparse Core Ops, SparseCore 0:
  8.9 25.3 all-gather.7
  35.8 31.5 all-gather.9
